TPU v7x, 32 devices: a whole 2x2x4 slice. The times are simulated.
32 devices in a mesh: groups: 1, row: 32 (over z, y, x, core).
Axes of the slice: x: 2, y: 2, z: 4, core: 2. Of those that a mesh axis runs over, the one named last changes fastest.
Arguments:
- pair_mantissa: bfloat16 [128, 128, 128], P(('groups', 'row')), may hold values from -6 to 6
- pair_exponent: int32 [128, 1, 128], P(('groups', 'row')), may hold values from -3 to 3
- residue_mask: int32 [128], P('groups'), may hold values 0 or 1
- ln_gain: float32 [128], replicated, may hold values from 0.25 to 1.75
- ln_shift: float32 [128], replicated, may hold values from -3 to 3
- w_proj: bfloat16 [128, 512], replicated, may hold values from -10 to 10
- w_bias: bfloat16 [128, 4], replicated, may hold values from -0.5 to 0.5
- gate_shift: float32 [128], replicated, may hold values from -4 to 4
- w_out: bfloat16 [128, 128], replicated, may hold values from -0.5 to 0.5
- out_shift: float32 [128], replicated, may hold values from -3 to 3
Outputs:
- update: bfloat16 [32, 128, 128], P(('groups', 'row'))
All inputs are finite; a program needn't handle non-finite values.
Results may differ from a plain program's by a relative error of at most 0.005.
Values may be sent and summed in bfloat16 or wider, within the bound.
A program may use at most 64 MiB of HBM per device.

v0:
```python
import jax
import jax.numpy as jnp
from jax import lax
from jax.sharding import PartitionSpec as P

WD = 1


epsilon = 1e-05
big_negative = 1000000000.0


def dequantize(mantissa, exponent):
    scaling = jnp.zeros(exponent.shape, jnp.float32)
    for expo_level in range(-3, 4):
        scaling = scaling + jnp.where(
            exponent == expo_level, jnp.float32(2.0**expo_level), jnp.float32(0.0)
        )
    row_count, block_count, channels = exponent.shape
    block_width = mantissa.shape[1] // block_count
    scaling = jnp.broadcast_to(
        scaling[:, :, None, :], (row_count, block_count, block_width, channels)
    )
    return mantissa.astype(jnp.float32) * scaling.reshape(
        row_count, block_count * block_width, channels
    )


def normalize(mantissa, exponent, ln_gain, ln_shift):
    values = dequantize(mantissa, exponent)
    center = jnp.mean(values, axis=-1, keepdims=True)
    spread = jnp.mean(jnp.square(values - center), axis=-1, keepdims=True)
    return ((values - center) * lax.rsqrt(spread + epsilon) * ln_gain + ln_shift).astype(
        jnp.bfloat16
    )


def project(columns, w_proj, gate_shift, inner_width, window_rows, head_size):
    key_value = jnp.einsum(
        "lmc,cd->mld",
        columns,
        w_proj[:, inner_width : 3 * inner_width],
        preferred_element_type=jnp.float32,
    ).astype(jnp.bfloat16)
    query_weight = jnp.concatenate([w_proj[:, :inner_width], w_proj[:, 3 * inner_width :]], axis=1)
    query_gate = jnp.einsum(
        "wmc,cd->mwd", columns[:window_rows], query_weight, preferred_element_type=jnp.float32
    )
    queries = (query_gate[..., :inner_width] * head_size ** (-0.5)).astype(jnp.bfloat16)
    gating = jax.nn.sigmoid(query_gate[..., inner_width:] + gate_shift)
    return (key_value, queries, gating)


def finish(gating, attended, w_out, out_shift):
    gated_out = (gating * attended).astype(jnp.bfloat16)
    return (
        jnp.einsum("mwd,dc->mwc", gated_out, w_out, preferred_element_type=jnp.float32) + out_shift
    ).astype(jnp.bfloat16)


def attend_whole(columns, key_bias, mask_bias, w_proj, gate_shift, w_out, out_shift):
    inner_width = w_out.shape[0]
    head_count = key_bias.shape[1]
    head_size = inner_width // head_count
    window_rows = key_bias.shape[2]
    key_value, queries, gating = project(
        columns, w_proj, gate_shift, inner_width, window_rows, head_size
    )

    def single_column(operands):
        kv_column, query_column = operands
        key_heads = kv_column[:, :inner_width].reshape(-1, head_count, head_size)
        value_heads = kv_column[:, inner_width:].reshape(-1, head_count, head_size)
        query_heads = query_column.reshape(window_rows, head_count, head_size)
        scores = jnp.einsum(
            "lhd,whd->lhw", key_heads, query_heads, preferred_element_type=jnp.float32
        )
        scores = scores + key_bias.astype(jnp.float32) + mask_bias[:, None, None]
        row_max = jnp.max(scores, axis=0)
        weights = jnp.exp(scores - row_max)
        denominator = jnp.sum(weights, axis=0)
        attended = jnp.einsum(
            "lhw,lhd->whd",
            weights.astype(jnp.bfloat16),
            value_heads,
            preferred_element_type=jnp.float32,
        )
        return (attended / denominator.T[:, :, None]).reshape(window_rows, inner_width)

    attended = lax.map(single_column, (key_value, queries))
    return finish(gating, attended, w_out, out_shift)


def per_device(
    pair_mantissa,
    pair_exponent,
    residue_mask,
    ln_gain,
    ln_shift,
    w_proj,
    w_bias,
    gate_shift,
    w_out,
    out_shift,
):
    devices_row = lax.axis_size("row")
    local_rows = pair_mantissa.shape[0]
    channels = pair_mantissa.shape[2]
    window_rows = WD * devices_row
    normal = normalize(pair_mantissa, pair_exponent, ln_gain, ln_shift)
    local_bias = jnp.einsum(
        "rwc,ch->rhw", normal[:, :window_rows], w_bias, preferred_element_type=jnp.float32
    ).astype(jnp.bfloat16)
    mask_bias = big_negative * (residue_mask.astype(jnp.float32) - 1.0)
    split_pair = normal.reshape(local_rows, devices_row, local_rows, channels)
    key_bias = lax.all_gather(local_bias, "row", axis=0, tiled=True)
    received = lax.all_to_all(split_pair, "row", split_axis=1, concat_axis=0, tiled=True)
    result = attend_whole(received[:, 0], key_bias, mask_bias, w_proj, gate_shift, w_out, out_shift)
    row_layout = lax.all_to_all(result, "row", split_axis=1, concat_axis=0, tiled=True)
    return jnp.transpose(row_layout, (1, 0, 2))


def solution(mesh):
    in_specs = (
        P(("groups", "row"), None, None),
        P(("groups", "row"), None, None),
        P("groups"),
        P(),
        P(),
        P(),
        P(),
        P(),
        P(),
        P(),
    )
    out_specs = P(("groups", "row"), None, None)
    return jax.shard_map(
        per_device, mesh=mesh, in_specs=in_specs, out_specs=out_specs, check_vma=False
    )
```

profile of v0, /device:TPU:0, one launch (start us, length us, event | category | flops | bytes accessed | tf_op | source)
XLA Modules:
  0.0 68.8 jit_solution(6774469167850363746)
XLA Ops:
  0.0 0.7 %fusion.32 = f32[4,1,128]{2,1,0:T(1,128)S(1)} fusion(s32[4,1,128]{2,1,0:T(1,128)} %param.13), kind=kLoop, calls=%fused_computation.53 | loop fusion | flops 10240 | bytes 4096 | tf_op jit(solution)/shard_map/add | solution.py:16
  0.7 1.1 %fusion.12 = f32[4,128]{1,0:T(4,128)S(1)} fusion(bf16[4,128,128]{2,1,0:T(8,128)(2,1)} %param.12, f32[4,128]{1,0:T(4,128)S(1)} %bitcast.76), kind=kLoop, calls=%fused_computation.24 | loop fusion | flops 196096 | bytes 135168 | tf_op jit(solution)/shard_map/reduce_sum | solution.py:31
  1.8 0.2 multiply_reduce_fusion
  2.1 0.6 copy-done.3
  2.7 0.2 add_convert_fusion
  2.9 0.7 %copy.18 = bf16[4,32,4,128]{3,0,2,1:T(4,128)(2,1)} copy(bf16[4,32,4,128]{3,2,1,0:T(4,128)(2,1)S(1)} %bitcast.72) | data formatting | bytes 262144 | tf_op jit(solution)/shard_map/reshape | solution.py:115
  3.7 7.3 %all-to-all-start = ((bf16[4,32,4,128]{3,0,2,1:T(4,128)(2,1)}), bf16[4,32,4,128]{3,0,2,1:T(4,128)(2,1)S(1)}, u32[]{:S(2)}, u32[]{:S(2)}) async-start(bf16[4,32,4,128]{3,0,2,1:T(4,128)(2,1)} %copy.18), calls=%async_computation | async-start | bytes 262144 | tf_op jit(solution)/shard_map/all_to_all | solution.py:117
  11.2 0.5 copy-done.6
  11.7 42.2 %all_gather.3 = bf16[128,4,32]{2,1,0:T(4,128)(2,1)S(1)} all-gather(bf16[4,4,32]{2,1,0:T(4,128)(2,1)S(1)} %fusion.10), channel_id=1, replica_groups=mesh['groups'=1,'row'=32] {'row'}, dimensions={0}, use_global_device_ids=true | all-gather | bytes 33792 | tf_op jit(solution)/shard_map/all_gather | solution.py:116
  54.3 0.2 fusion.8
  54.6 3.8 %while.10 = (s32[]{:T(128)}, f32[4,32,128]{2,1,0:T(8,128)S(1)}, bf16[4,128,256]{2,1,0:T(8,128)(2,1)S(1)}, bf16[4,32,128]{2,1,0:T(8,128)(2,1)S(1)}, bf16[128,4,32...) while((s32[]{:T(128)}, f32[4,32,128]{2,1,0:T(8,128)S(1)}, bf16[4,128,256]{2,1,0:T(8,128)(2,1)S(1)}, ...), condition=%wide.region_5.6_spmd, body=%wide.region_2.5_spmd.sunk | while | flops 2232066 | bytes 814169 | solution.py:90
  54.8 0.2 fusion.54
  55.0 0.2 fusion.55
  55.2 0.2 fusion.56
  55.8 0.2 fusion.54
  56.0 0.2 fusion.55
  56.2 0.2 fusion.56
  56.7 0.2 fusion.54
  57.1 0.2 fusion.56
  57.7 0.2 fusion.54
  58.1 0.2 fusion.56
  58.4 0.6 copy-done.7
  59.2 9.0 %all_to_all.30 = bf16[4,32,128]{2,0,1:T(4,128)(2,1)S(1)} all-to-all(bf16[4,32,128]{2,0,1:T(4,128)(2,1)S(1)} %copy.24), channel_id=1, replica_groups=mesh['groups'=1,'row'=32] {'row'}, dimensions={1} | all-to-all | bytes 65536 | tf_op jit(solution)/shard_map/all_to_all | solution.py:119
  68.2 0.6 copy.50
  (60 shorter events, 2.3 us)
Async XLA Ops:
  0.0 58.4 %copy-start = (bf16[128,128]{1,0:T(8,128)(2,1)S(1)}, bf16[128,128]{1,0:T(8,128)(2,1)}, u32[]{:S(2)}) copy-start(bf16[128,128]{1,0:T(8,128)(2,1)} %param.20) | copy-start | bytes 98308
  0.0 1.8 %copy-start.1 = (bf16[4,128,128]{2,1,0:T(8,128)(2,1)S(1)}, bf16[4,128,128]{2,1,0:T(8,128)(2,1)}, u32[]{:S(2)}) copy-start(bf16[4,128,128]{2,1,0:T(8,128)(2,1)} %param.12) | copy-start | bytes 393220
  2.1 0.7 copy-start.3
  2.1 0.7 copy-start.4
  3.7 7.3 %copy-start.5 = (bf16[128,4]{0,1:T(4,128)(2,1)S(1)}, bf16[128,4]{0,1:T(4,128)(2,1)}, u32[]{:S(2)}) copy-start(bf16[128,4]{0,1:T(4,128)(2,1)} %param.18) | copy-start | bytes 3076
  3.7 50.4 %all-to-all-start = ((bf16[4,32,4,128]{3,0,2,1:T(4,128)(2,1)}), bf16[4,32,4,128]{3,0,2,1:T(4,128)(2,1)S(1)}, u32[]{:S(2)}, u32[]{:S(2)}) async-start(bf16[4,32,4,128]{3,0,2,1:T(4,128)(2,1)} %copy.18), calls=%async_computation | async-start | bytes 262144 | tf_op jit(solution)/shard_map/all_to_all | solution.py:117
  11.0 0.7 copy-start.6
  11.7 42.3 %copy-start.2 = (bf16[128,512]{1,0:T(8,128)(2,1)S(1)}, bf16[128,512]{1,0:T(8,128)(2,1)}, u32[]{:S(2)}) copy-start(bf16[128,512]{1,0:T(8,128)(2,1)} %param.17) | copy-start | bytes 393220
  58.3 0.7 copy-start.7
  58.4 0.7 copy-start.8
where the time goes:
time: 69 us; the launch traced here: 68.8 us
  blocking collectives  51.2 us (74%)
  starting transfers between devices  7.33 us (11%)
  local copies, waits for them, and re-layouts  4.59 us (7%)
  other arithmetic  2.97 us (4%)
  matrix products  2.33 us (3%)
    all_gather x1, blocking collectives, per_device(): key_bias = lax.all_gather(local_bias, 'row', axis=0, tiled=True)  42.2 us
    all_to_all x1, blocking collectives, per_device(): lax.all_to_all(result, 'row', split_axis=1, concat_axis=0, tiled=True)  8.95 us
    all_to_all x1, starting transfers between devices, per_device(): lax.all_to_all(split_pair, 'row', split_axis=1, concat_axis=0, tiled=True)  7.33 us
    unnamed x19, local copies, waits for them, and re-layouts  2.47 us
  transfers between devices with their start and end apart: 1, of which 0 were waited for; matrix products, arithmetic and copies ran while one was open for 0% of the time, Pallas kernels for 0%

commit v1 on v0

v1 whole, which is shorter than its diff:
```python
import functools

import jax
import jax.numpy as jnp
from jax import lax
from jax.experimental import pallas as pl
from jax.experimental.pallas import tpu as pltpu
from jax.sharding import PartitionSpec as P

WD = 1

epsilon = 1e-05
big_negative = 1000000000.0
MESH = pl.DeviceIdType.MESH
F32 = jnp.float32
BF16 = jnp.bfloat16


def dot(a, b, ca=1, cb=0):
    return lax.dot_general(a, b, (((ca,), (cb,)), ((), ())), preferred_element_type=F32)


def head_mask(rows, lanes, row_group, lane_group):
    row_head = lax.broadcasted_iota(jnp.int32, (rows, lanes), 0) // row_group
    lane_head = lax.broadcasted_iota(jnp.int32, (rows, lanes), 1) // lane_group
    return row_head == lane_head


def each_peer(n, body):
    if n <= 32:
        for step in range(1, n):
            body(step)
    else:
        lax.fori_loop(1, n, lambda step, _: (body(step), 0)[1], 0)


def kernel(
    n, heads,
    mant_hbm, expo_hbm, mask_hbm, gain_hbm, shift_hbm, proj_hbm, wbias_hbm, gate_hbm, wout_hbm, oshift_hbm,
    out_ref,
    mant, expo, mask, gain, shift, proj, wbias, gate, wout, oshift,
    send, recv, bias_send, bias_recv, rows, mixed, back,
    load_sems, send_sems, recv_sems,
):
    me = lax.axis_index("row")
    local, length, channels = mant.shape
    inner = wout.shape[0]
    window = WD * n
    size = inner // heads
    lanes = heads * window

    barrier = pltpu.get_barrier_semaphore()
    loads = [
        pltpu.make_async_copy(src, dst, load_sems.at[number])
        for number, (src, dst) in enumerate(
            [
                (mant_hbm, mant), (expo_hbm, expo), (gain_hbm, gain), (shift_hbm, shift), (wbias_hbm, wbias),
                (mask_hbm, mask), (proj_hbm, proj), (gate_hbm, gate), (wout_hbm, wout), (oshift_hbm, oshift),
            ]
        )
    ]
    for load in loads:
        load.start()

    def greet(step):
        pl.semaphore_signal(barrier, inc=1, device_id={"row": lax.rem(me + step, n)}, device_id_type=MESH)

    each_peer(n, greet)

    for load in loads[:5]:
        load.wait()
    exponent = expo[...]
    scaling = jnp.zeros(exponent.shape, F32)
    for level in range(-3, 4):
        scaling = scaling + jnp.where(exponent == level, F32(2.0**level), F32(0.0))
    blocks = exponent.shape[1]
    values = mant[...].astype(F32).reshape(local, blocks, length // blocks, channels) * scaling[:, :, None, :]
    values = values.reshape(local * length, channels)
    center = jnp.mean(values, axis=-1, keepdims=True)
    values = values - center
    spread = jnp.mean(jnp.square(values), axis=-1, keepdims=True)
    normal = values * lax.rsqrt(spread + epsilon) * gain[...] + shift[...]

    split = normal.reshape(local, length // 8, 8, channels)
    low = lax.broadcasted_iota(jnp.int32, (length // 8, 8, channels), 1) < local
    even, odd = [], []
    for pair in range(0, local, 2):
        one, two = split[pair], split[pair + 1]
        even.append(jnp.where(low, one, pltpu.roll(two, local, 1)))
        odd.append(jnp.where(low, pltpu.roll(one, local, 1), two))
    send[:, 0] = jnp.concatenate(even, axis=1).astype(BF16)
    send[:, 1] = jnp.concatenate(odd, axis=1).astype(BF16)

    rounded = normal.astype(BF16).reshape(local, length, channels)
    bias_mask = head_mask(heads, lanes, 1, window)
    local_bias = []
    for row in range(local):
        repeated = jnp.concatenate([rounded[row, :window]] * heads, axis=0)
        product = dot(wbias[...], repeated, 1, 1)
        local_bias.append(jnp.sum(jnp.where(bias_mask, product, 0.0), axis=0, keepdims=True))
    bias_send[...] = jnp.concatenate(local_bias, axis=0).astype(BF16)

    for load in loads[5:]:
        load.wait()
    mask_row = big_negative * (mask[...].astype(F32) - 1.0)
    mask_column = jnp.broadcast_to(mask_row, (128, length)).T[:, :1]

    pl.semaphore_wait(barrier, n - 1)

    def pair_of(peer):
        return peer // 2, lax.rem(peer, 2)

    def scatter(step):
        peer = lax.rem(me + step, n)
        high, parity = pair_of(peer)
        pltpu.make_async_remote_copy(
            src_ref=send.at[high, parity], dst_ref=recv.at[me],
            send_sem=send_sems.at[0], recv_sem=recv_sems.at[0],
            device_id={"row": peer}, device_id_type=MESH,
        ).start()

    def spread_bias(step):
        peer = lax.rem(me + step, n)
        pltpu.make_async_remote_copy(
            src_ref=bias_send, dst_ref=bias_recv.at[me],
            send_sem=send_sems.at[1], recv_sem=recv_sems.at[1],
            device_id={"row": peer}, device_id_type=MESH,
        ).start()

    each_peer(n, scatter)
    each_peer(n, spread_bias)
    high, parity = pair_of(me)
    recv[me] = send[high, parity]
    bias_recv[me] = bias_send[...]

    def wait_all(ref, semaphore):
        whole = ref.at[pl.ds(0, n - 1)]
        pltpu.make_async_copy(whole, whole, semaphore).wait()

    wait_all(recv, recv_sems.at[0])
    wait_all(bias_recv, recv_sems.at[1])

    rows[...] = recv[...].astype(F32).reshape(n * local * local, channels)
    keys_count = n * local
    columns = [rows[pl.ds(column, keys_count, stride=local), :].astype(BF16) for column in range(local)]
    bias = bias_recv[...].astype(F32).reshape(keys_count, lanes)
    query_mask = head_mask(lanes, inner, window, size)
    key_value = dot(jnp.concatenate(columns, axis=0), proj[:, inner : 3 * inner]).astype(BF16)
    tops = jnp.concatenate([column[:window] for column in columns], axis=0)
    queries = dot(tops, proj[:, :inner]) * size ** (-0.5)
    gating = jax.nn.sigmoid(dot(tops, proj[:, 3 * inner :]) + gate[...])
    attended = []
    for column in range(local):
        keys = key_value[column * keys_count : (column + 1) * keys_count, :inner]
        held = key_value[column * keys_count : (column + 1) * keys_count, inner:]
        query = queries[column * window : (column + 1) * window]
        query = jnp.where(query_mask, jnp.concatenate([query] * heads, axis=0), 0.0).astype(BF16)
        scores = dot(keys, query, 1, 1) + bias + mask_column
        weights = jnp.exp(scores - jnp.max(scores, axis=0, keepdims=True))
        totals = jnp.sum(weights, axis=0, keepdims=True)
        weights = (weights / totals).astype(BF16)
        mixture = jnp.where(query_mask, dot(weights, held, 0, 0), 0.0)
        attended.append(jnp.sum(mixture.reshape(heads, window, inner), axis=0))
    gated = (gating * jnp.concatenate(attended, axis=0)).astype(BF16)
    update = dot(gated, wout[...]) + oshift[...]
    for column in range(local):
        mixed[pl.ds(column, window, stride=local), :] = update[column * window : (column + 1) * window]
    back[...] = mixed[...].reshape(n, WD * local, channels).astype(BF16)

    def give_back(step):
        peer = lax.rem(me + step, n)
        pltpu.make_async_remote_copy(
            src_ref=back.at[peer], dst_ref=out_ref.at[me],
            send_sem=send_sems.at[2], recv_sem=recv_sems.at[2],
            device_id={"row": peer}, device_id_type=MESH,
        ).start()

    each_peer(n, give_back)
    out_ref[me] = back[me]
    wait_all(out_ref, recv_sems.at[2])
    wait_all(recv, send_sems.at[0])
    wait_all(bias_recv, send_sems.at[1])
    wait_all(out_ref, send_sems.at[2])


def per_device(
    pair_mantissa,
    pair_exponent,
    residue_mask,
    ln_gain,
    ln_shift,
    w_proj,
    w_bias,
    gate_shift,
    w_out,
    out_shift,
):
    n = lax.axis_size("row")
    local, length, channels = pair_mantissa.shape
    heads = w_bias.shape[1]
    lanes = heads * WD * n
    args = (
        pair_mantissa, pair_exponent, residue_mask[None], ln_gain[None], ln_shift[None],
        w_proj, w_bias.T, gate_shift[None], w_out, out_shift[None],
    )
    result = pl.pallas_call(
        functools.partial(kernel, n, heads),
        out_shape=jax.ShapeDtypeStruct((n, WD * local, channels), BF16),
        in_specs=[pl.BlockSpec(memory_space=pl.ANY)] * len(args),
        out_specs=pl.BlockSpec(memory_space=pltpu.VMEM),
        scratch_shapes=[pltpu.VMEM(arg.shape, arg.dtype) for arg in args]
        + [
            pltpu.VMEM((n // 2, 2, local * local, channels), BF16),
            pltpu.VMEM((n, local * local, channels), BF16),
            pltpu.VMEM((local, lanes), BF16),
            pltpu.VMEM((n, local, lanes), BF16),
            pltpu.VMEM((n * local * local, channels), F32),
            pltpu.VMEM((n * WD * local, channels), F32),
            pltpu.VMEM((n, WD * local, channels), BF16),
            pltpu.SemaphoreType.DMA((len(args),)),
            pltpu.SemaphoreType.DMA((3,)),
            pltpu.SemaphoreType.DMA((3,)),
        ],
        compiler_params=pltpu.CompilerParams(collective_id=0, has_side_effects=True),
    )(*args)
    return result.reshape(WD, length, channels)


def solution(mesh):
    in_specs = (
        P(("groups", "row"), None, None),
        P(("groups", "row"), None, None),
        P("groups"),
        P(),
        P(),
        P(),
        P(),
        P(),
        P(),
        P(),
    )
    out_specs = P(("groups", "row"), None, None)
    return jax.shard_map(
        per_device, mesh=mesh, in_specs=in_specs, out_specs=out_specs, check_vma=False
    )
```

time: 69 us -> 21.1 us (0.31)
  blocking collectives: 51.2 us -> 0 us
  Pallas kernels: 0 us -> 19.5 us
  starting transfers between devices: 7.33 us -> 0 us
  local copies, waits for them, and re-layouts: 4.59 us -> 1.38 us
  other arithmetic: 2.97 us -> 0 us
  matrix products: 2.33 us -> 0 us
    all_gather x1 -> x0, blocking collectives: 42.2 us -> none  [per_device(): key_bias = lax.all_gather(local_bias, 'row', axis=0, tiled=True)]
    pallas_call x0 -> x1, Pallas kernels: none -> 19.5 us  [per_device(): pl.pallas_call(functools.partial(kernel, n, heads), out_shape=jax.ShapeDt...]
    all_to_all x1 -> x0, blocking collectives: 8.95 us -> none  [per_device(): lax.all_to_all(result, 'row', split_axis=1, concat_axis=0, tiled=True)]
    all_to_all x1 -> x0, starting transfers between devices: 7.33 us -> none  [per_device(): lax.all_to_all(split_pair, 'row', split_axis=1, concat_axis=0, tiled=True)]
    dot_general x12 -> x0, matrix products: 2.33 us -> none  [the longest x4 0.84 us: single_column(): jnp.einsum('lhd,whd->lhw', key_heads, query_heads, preferred_element_type...]
    reduce_sum x6 -> x0, other arithmetic: 2.01 us -> none  [the longest x1 1.05 us: normalize(): center = jnp.mean(values, axis=-1, keepdims=True)]
    unnamed x19 -> x1, local copies, waits for them, and re-layouts: 2.47 us -> 1.38 us
    reshape x5 -> x0, local copies, waits for them, and re-layouts: 1.08 us -> none  [the longest x1 0.75 us: per_device(): split_pair = normal.reshape(local_rows, devices_row, local_rows, channels)]
  transfers between devices with their start and end apart: 1 -> 0, of which waited for: 0 -> 0; matrix products, arithmetic and copies ran while one was open for 0% -> 0% of each run, Pallas kernels for 0% -> 0%
where the time goes in v1:
time: 21.1 us; the launch traced here: 20.9 us
  Pallas kernels  19.5 us (92%)
  local copies, waits for them, and re-layouts  1.38 us (7%)
    pallas_call x1, Pallas kernels, per_device(): pl.pallas_call(functools.partial(kernel, n, heads), out_shape=jax.ShapeDt...  19.5 us
    unnamed x1, local copies, waits for them, and re-layouts  1.38 us

profile of v1, /device:TPU:0, one launch (start us, length us, event | category | flops | bytes accessed | tf_op | source)
XLA Modules:
  0.0 20.9 jit_solution(3638050748359611028)
XLA Ops:
  0.0 19.5 %shard_map.100 = bf16[32,4,128]{2,1,0:T(4,128)(2,1)} custom-call(bf16[4,128,128]{2,1,0:T(8,128)(2,1)} %mant_hbm.1, s32[4,1,128]{2,1,0:T(1,128)} %expo_hbm.1, s32[1,128]{1,0:T(1,128)} %bitcast.9, f32[1,128]{1,0:T(1,128)} %bitcast.10, f32[1,128]{1,0:T(1,128)} %bitcast.11, bf16[128,512]{1,0:T(8,128)(2,1)} %proj_hbm.1, bf16[4,128]{1,0:T(4,128)(2,1)} %bitcast.8, ...), custom_call_target="tpu_custom_call" | custom-call | tf_op jit(solution)/shard_map/pallas_call | solution.py:206
  19.5 1.4 %copy.12 = bf16[1,128,128]{2,1,0:T(8,128)(2,1)} copy(bf16[1,128,128]{2,1,0:T(8,128)(2,1)} %bitcast.7) | data formatting | bytes 65536

commit v2 on v1

--- a/solution.py
+++ b/solution.py
@@ -11,7 +11,7 @@
 
 epsilon = 1e-05
 big_negative = 1000000000.0
-MESH = pl.DeviceIdType.MESH
+LOGICAL = pl.DeviceIdType.LOGICAL
 F32 = jnp.float32
 BF16 = jnp.bfloat16
 
@@ -27,11 +27,8 @@
 
 
 def each_peer(n, body):
-    if n <= 32:
-        for step in range(1, n):
-            body(step)
-    else:
-        lax.fori_loop(1, n, lambda step, _: (body(step), 0)[1], 0)
+    for step in range(n - 1, 0, -1):
+        body(step)
 
 
 def kernel(
@@ -43,6 +40,16 @@
     load_sems, send_sems, recv_sems,
 ):
     me = lax.axis_index("row")
+    base = lax.axis_index("groups") * n
+
+    flips, rest = [], me
+    while len(flips) < (n - 1).bit_length():
+        flips.append((1 - 2 * lax.rem(rest, 2)) * 2 ** len(flips))
+        rest = rest // 2
+
+    def peer_of(step):
+        return me + sum(flip for bit, flip in enumerate(flips) if step >> bit & 1)
+
     local, length, channels = mant.shape
     inner = wout.shape[0]
     window = WD * n
@@ -50,6 +57,12 @@
     lanes = heads * window
 
     barrier = pltpu.get_barrier_semaphore()
+
+    def greet(step):
+        pl.semaphore_signal(barrier, inc=1, device_id=base + peer_of(step), device_id_type=LOGICAL)
+
+    each_peer(n, greet)
+
     loads = [
         pltpu.make_async_copy(src, dst, load_sems.at[number])
         for number, (src, dst) in enumerate(
@@ -61,11 +74,6 @@
     ]
     for load in loads:
         load.start()
-
-    def greet(step):
-        pl.semaphore_signal(barrier, inc=1, device_id={"row": lax.rem(me + step, n)}, device_id_type=MESH)
-
-    each_peer(n, greet)
 
     for load in loads[:5]:
         load.wait()
@@ -88,8 +96,8 @@
         one, two = split[pair], split[pair + 1]
         even.append(jnp.where(low, one, pltpu.roll(two, local, 1)))
         odd.append(jnp.where(low, pltpu.roll(one, local, 1), two))
-    send[:, 0] = jnp.concatenate(even, axis=1).astype(BF16)
-    send[:, 1] = jnp.concatenate(odd, axis=1).astype(BF16)
+    pairs = jnp.stack([jnp.concatenate(even, axis=1), jnp.concatenate(odd, axis=1)], axis=1)
+    send[...] = pairs.reshape(n, local * local, channels).astype(BF16)
 
     rounded = normal.astype(BF16).reshape(local, length, channels)
     bias_mask = head_mask(heads, lanes, 1, window)
@@ -107,30 +115,25 @@
 
     pl.semaphore_wait(barrier, n - 1)
 
-    def pair_of(peer):
-        return peer // 2, lax.rem(peer, 2)
-
     def scatter(step):
-        peer = lax.rem(me + step, n)
-        high, parity = pair_of(peer)
+        peer = peer_of(step)
         pltpu.make_async_remote_copy(
-            src_ref=send.at[high, parity], dst_ref=recv.at[me],
+            src_ref=send.at[peer], dst_ref=recv.at[me],
             send_sem=send_sems.at[0], recv_sem=recv_sems.at[0],
-            device_id={"row": peer}, device_id_type=MESH,
+            device_id=base + peer, device_id_type=LOGICAL,
         ).start()
 
     def spread_bias(step):
-        peer = lax.rem(me + step, n)
+        peer = peer_of(step)
         pltpu.make_async_remote_copy(
             src_ref=bias_send, dst_ref=bias_recv.at[me],
             send_sem=send_sems.at[1], recv_sem=recv_sems.at[1],
-            device_id={"row": peer}, device_id_type=MESH,
+            device_id=base + peer, device_id_type=LOGICAL,
         ).start()
 
     each_peer(n, scatter)
     each_peer(n, spread_bias)
-    high, parity = pair_of(me)
-    recv[me] = send[high, parity]
+    recv[me] = send[me]
     bias_recv[me] = bias_send[...]
 
     def wait_all(ref, semaphore):
@@ -138,17 +141,17 @@
         pltpu.make_async_copy(whole, whole, semaphore).wait()
 
     wait_all(recv, recv_sems.at[0])
-    wait_all(bias_recv, recv_sems.at[1])
 
     rows[...] = recv[...].astype(F32).reshape(n * local * local, channels)
     keys_count = n * local
     columns = [rows[pl.ds(column, keys_count, stride=local), :].astype(BF16) for column in range(local)]
-    bias = bias_recv[...].astype(F32).reshape(keys_count, lanes)
     query_mask = head_mask(lanes, inner, window, size)
     key_value = dot(jnp.concatenate(columns, axis=0), proj[:, inner : 3 * inner]).astype(BF16)
     tops = jnp.concatenate([column[:window] for column in columns], axis=0)
     queries = dot(tops, proj[:, :inner]) * size ** (-0.5)
     gating = jax.nn.sigmoid(dot(tops, proj[:, 3 * inner :]) + gate[...])
+    wait_all(bias_recv, recv_sems.at[1])
+    bias = bias_recv[...].astype(F32).reshape(keys_count, lanes)
     attended = []
     for column in range(local):
         keys = key_value[column * keys_count : (column + 1) * keys_count, :inner]
@@ -168,11 +171,11 @@
     back[...] = mixed[...].reshape(n, WD * local, channels).astype(BF16)
 
     def give_back(step):
-        peer = lax.rem(me + step, n)
+        peer = peer_of(step)
         pltpu.make_async_remote_copy(
             src_ref=back.at[peer], dst_ref=out_ref.at[me],
             send_sem=send_sems.at[2], recv_sem=recv_sems.at[2],
-            device_id={"row": peer}, device_id_type=MESH,
+            device_id=base + peer, device_id_type=LOGICAL,
         ).start()
 
     each_peer(n, give_back)
@@ -205,12 +208,12 @@
     )
     result = pl.pallas_call(
         functools.partial(kernel, n, heads),
-        out_shape=jax.ShapeDtypeStruct((n, WD * local, channels), BF16),
+        out_shape=pltpu.VMEM((n, WD * local, channels), BF16),
         in_specs=[pl.BlockSpec(memory_space=pl.ANY)] * len(args),
         out_specs=pl.BlockSpec(memory_space=pltpu.VMEM),
         scratch_shapes=[pltpu.VMEM(arg.shape, arg.dtype) for arg in args]
         + [
-            pltpu.VMEM((n // 2, 2, local * local, channels), BF16),
+            pltpu.VMEM((n, local * local, channels), BF16),
             pltpu.VMEM((n, local * local, channels), BF16),
             pltpu.VMEM((local, lanes), BF16),
             pltpu.VMEM((n, local, lanes), BF16),

time: 21.1 us -> 19.3 us (0.915)
  Pallas kernels: 19.5 us -> 18.5 us
  local copies, waits for them, and re-layouts: 1.38 us -> 0.62 us
    pallas_call x1, Pallas kernels: 19.5 us -> 18.5 us  [per_device(): pl.pallas_call(functools.partial(kernel, n, heads), out_shape=pltpu.VMEM(...]
    unnamed x1, local copies, waits for them, and re-layouts: 1.38 us -> 0.62 us
where the time goes in v2:
time: 19.3 us; the launch traced here: 19.1 us
  Pallas kernels  18.5 us (96%)
  local copies, waits for them, and re-layouts  0.62 us (3%)
    pallas_call x1, Pallas kernels, per_device(): pl.pallas_call(functools.partial(kernel, n, heads), out_shape=pltpu.VMEM(...  18.5 us
    unnamed x1, local copies, waits for them, and re-layouts  0.62 us

profile of v2, /device:TPU:0, one launch (start us, length us, event | category | flops | bytes accessed | tf_op | source)
XLA Modules:
  0.0 19.1 jit_solution(1112398056153343944)
XLA Ops:
  0.0 18.5 %shard_map.100 = bf16[32,4,128]{2,1,0:T(4,128)(2,1)S(1)} custom-call(bf16[4,128,128]{2,1,0:T(8,128)(2,1)} %mant_hbm.1, s32[4,1,128]{2,1,0:T(1,128)} %expo_hbm.1, s32[1,128]{1,0:T(1,128)} %bitcast.9, f32[1,128]{1,0:T(1,128)} %bitcast.10, f32[1,128]{1,0:T(1,128)} %bitcast.11, bf16[128,512]{1,0:T(8,128)(2,1)} %proj_hbm.1, bf16[4,128]{1,0:T(4,128)(2,1)} %bitcast.8, ...), custom_call_target="tpu_custom_call" | custom-call | tf_op jit(solution)/shard_map/pallas_call | solution.py:209
  18.5 0.6 %copy.12 = bf16[1,128,128]{2,1,0:T(8,128)(2,1)} copy(bf16[1,128,128]{2,1,0:T(8,128)(2,1)S(1)} %bitcast.7) | data formatting | bytes 65536

commit v3 on v2

--- a/solution.py
+++ b/solution.py
@@ -37,7 +37,7 @@
     out_ref,
     mant, expo, mask, gain, shift, proj, wbias, gate, wout, oshift,
     send, recv, bias_send, bias_recv, rows, mixed, back,
-    load_sems, send_sems, recv_sems,
+    load_sems, send_sems, recv_sems, swap_sems,
 ):
     me = lax.axis_index("row")
     base = lax.axis_index("groups") * n
@@ -126,20 +126,30 @@
     def spread_bias(step):
         peer = peer_of(step)
         pltpu.make_async_remote_copy(
-            src_ref=bias_send, dst_ref=bias_recv.at[me],
+            src_ref=bias_send, dst_ref=bias_recv.at[lax.rem(me, 2), me // 2],
             send_sem=send_sems.at[1], recv_sem=recv_sems.at[1],
             device_id=base + peer, device_id_type=LOGICAL,
         ).start()
 
+    for step in range(n - 2, 0, -2):
+        spread_bias(step)
     each_peer(n, scatter)
-    each_peer(n, spread_bias)
     recv[me] = send[me]
-    bias_recv[me] = bias_send[...]
+    bias_recv[lax.rem(me, 2), me // 2] = bias_send[...]
 
     def wait_all(ref, semaphore):
         whole = ref.at[pl.ds(0, n - 1)]
         pltpu.make_async_copy(whole, whole, semaphore).wait()
 
+    mine, others = lax.rem(me, 2), 1 - lax.rem(me, 2)
+    most = bias_recv.at[0, pl.ds(0, n // 2 - 1)]
+    pltpu.make_async_copy(most, most, recv_sems.at[1]).wait()
+    swap = pltpu.make_async_remote_copy(
+        src_ref=bias_recv.at[mine], dst_ref=bias_recv.at[mine],
+        send_sem=swap_sems.at[0], recv_sem=swap_sems.at[1],
+        device_id=base + peer_of(1), device_id_type=LOGICAL,
+    )
+    swap.start()
     wait_all(recv, recv_sems.at[0])
 
     rows[...] = recv[...].astype(F32).reshape(n * local * local, channels)
@@ -150,8 +160,8 @@
     tops = jnp.concatenate([column[:window] for column in columns], axis=0)
     queries = dot(tops, proj[:, :inner]) * size ** (-0.5)
     gating = jax.nn.sigmoid(dot(tops, proj[:, 3 * inner :]) + gate[...])
-    wait_all(bias_recv, recv_sems.at[1])
-    bias = bias_recv[...].astype(F32).reshape(keys_count, lanes)
+    swap.wait()
+    bias = jnp.stack([bias_recv[0], bias_recv[1]], axis=1).astype(F32).reshape(keys_count, lanes)
     attended = []
     for column in range(local):
         keys = key_value[column * keys_count : (column + 1) * keys_count, :inner]
@@ -161,7 +171,7 @@
         scores = dot(keys, query, 1, 1) + bias + mask_column
         weights = jnp.exp(scores - jnp.max(scores, axis=0, keepdims=True))
         totals = jnp.sum(weights, axis=0, keepdims=True)
-        weights = (weights / totals).astype(BF16)
+        weights = (weights * (1.0 / totals)).astype(BF16)
         mixture = jnp.where(query_mask, dot(weights, held, 0, 0), 0.0)
         attended.append(jnp.sum(mixture.reshape(heads, window, inner), axis=0))
     gated = (gating * jnp.concatenate(attended, axis=0)).astype(BF16)
@@ -182,7 +192,7 @@
     out_ref[me] = back[me]
     wait_all(out_ref, recv_sems.at[2])
     wait_all(recv, send_sems.at[0])
-    wait_all(bias_recv, send_sems.at[1])
+    pltpu.make_async_copy(most, most, send_sems.at[1]).wait()
     wait_all(out_ref, send_sems.at[2])
 
 
@@ -216,13 +226,14 @@
             pltpu.VMEM((n, local * local, channels), BF16),
             pltpu.VMEM((n, local * local, channels), BF16),
             pltpu.VMEM((local, lanes), BF16),
-            pltpu.VMEM((n, local, lanes), BF16),
+            pltpu.VMEM((2, n // 2, local, lanes), BF16),
             pltpu.VMEM((n * local * local, channels), F32),
             pltpu.VMEM((n * WD * local, channels), F32),
             pltpu.VMEM((n, WD * local, channels), BF16),
             pltpu.SemaphoreType.DMA((len(args),)),
             pltpu.SemaphoreType.DMA((3,)),
             pltpu.SemaphoreType.DMA((3,)),
+            pltpu.SemaphoreType.DMA((2,)),
         ],
         compiler_params=pltpu.CompilerParams(collective_id=0, has_side_effects=True),
     )(*args)

time: 19.3 us -> 18.9 us (0.979)
  Pallas kernels: 18.5 us -> 18.2 us
    pallas_call x1, Pallas kernels: 18.5 us -> 18.2 us  [per_device(): pl.pallas_call(functools.partial(kernel, n, heads), out_shape=pltpu.VMEM(...]
where the time goes in v3:
time: 18.9 us; the launch traced here: 18.8 us
  Pallas kernels  18.2 us (96%)
  local copies, waits for them, and re-layouts  0.62 us (3%)
    pallas_call x1, Pallas kernels, per_device(): pl.pallas_call(functools.partial(kernel, n, heads), out_shape=pltpu.VMEM(...  18.2 us
    unnamed x1, local copies, waits for them, and re-layouts  0.62 us

profile of v3, /device:TPU:0, one launch (start us, length us, event | category | flops | bytes accessed | tf_op | source)
XLA Modules:
  0.0 18.8 jit_solution(8318493854645528786)
XLA Ops:
  0.0 18.2 %shard_map.100 = bf16[32,4,128]{2,1,0:T(4,128)(2,1)S(1)} custom-call(bf16[4,128,128]{2,1,0:T(8,128)(2,1)} %mant_hbm.1, s32[4,1,128]{2,1,0:T(1,128)} %expo_hbm.1, s32[1,128]{1,0:T(1,128)} %bitcast.9, f32[1,128]{1,0:T(1,128)} %bitcast.10, f32[1,128]{1,0:T(1,128)} %bitcast.11, bf16[128,512]{1,0:T(8,128)(2,1)} %proj_hbm.1, bf16[4,128]{1,0:T(4,128)(2,1)} %bitcast.8, ...), custom_call_target="tpu_custom_call" | custom-call | tf_op jit(solution)/shard_map/pallas_call | solution.py:219
  18.2 0.6 %copy.12 = bf16[1,128,128]{2,1,0:T(8,128)(2,1)} copy(bf16[1,128,128]{2,1,0:T(8,128)(2,1)S(1)} %bitcast.7) | data formatting | bytes 65536

commit v4 on v3

--- a/solution.py
+++ b/solution.py
@@ -119,7 +119,7 @@
         peer = peer_of(step)
         pltpu.make_async_remote_copy(
             src_ref=send.at[peer], dst_ref=recv.at[me],
-            send_sem=send_sems.at[0], recv_sem=recv_sems.at[0],
+            send_sem=send_sems.at[0], recv_sem=recv_sems.at[0 if step < n // 2 else 3],
             device_id=base + peer, device_id_type=LOGICAL,
         ).start()
 
@@ -141,7 +141,7 @@
         whole = ref.at[pl.ds(0, n - 1)]
         pltpu.make_async_copy(whole, whole, semaphore).wait()
 
-    mine, others = lax.rem(me, 2), 1 - lax.rem(me, 2)
+    mine = lax.rem(me, 2)
     most = bias_recv.at[0, pl.ds(0, n // 2 - 1)]
     pltpu.make_async_copy(most, most, recv_sems.at[1]).wait()
     swap = pltpu.make_async_remote_copy(
@@ -150,9 +150,12 @@
         device_id=base + peer_of(1), device_id_type=LOGICAL,
     )
     swap.start()
-    wait_all(recv, recv_sems.at[0])
-
-    rows[...] = recv[...].astype(F32).reshape(n * local * local, channels)
+    half, count = me // (n // 2), n // 2 * local * local
+    for number, part in ((0, half), (3, 1 - half)):
+        expected = recv.at[pl.ds(0, n // 2 - (number == 0))]
+        pltpu.make_async_copy(expected, expected, recv_sems.at[number]).wait()
+        arrived = recv[pl.ds(part * (n // 2), n // 2)]
+        rows[pl.ds(pl.multiple_of(part * count, count), count), :] = arrived.astype(F32).reshape(count, channels)
     keys_count = n * local
     columns = [rows[pl.ds(column, keys_count, stride=local), :].astype(BF16) for column in range(local)]
     query_mask = head_mask(lanes, inner, window, size)
@@ -190,10 +193,10 @@
 
     each_peer(n, give_back)
     out_ref[me] = back[me]
-    wait_all(out_ref, recv_sems.at[2])
     wait_all(recv, send_sems.at[0])
     pltpu.make_async_copy(most, most, send_sems.at[1]).wait()
     wait_all(out_ref, send_sems.at[2])
+    wait_all(out_ref, recv_sems.at[2])
 
 
 def per_device(
@@ -232,7 +235,7 @@
             pltpu.VMEM((n, WD * local, channels), BF16),
             pltpu.SemaphoreType.DMA((len(args),)),
             pltpu.SemaphoreType.DMA((3,)),
-            pltpu.SemaphoreType.DMA((3,)),
+            pltpu.SemaphoreType.DMA((4,)),
             pltpu.SemaphoreType.DMA((2,)),
         ],
         compiler_params=pltpu.CompilerParams(collective_id=0, has_side_effects=True),

time: 18.9 us -> 18.9 us (level)
  no operation moved by 1% of the time
where the time goes in v4:
time: 18.9 us; the launch traced here: 18.8 us
  Pallas kernels  18.2 us (96%)
  local copies, waits for them, and re-layouts  0.62 us (3%)
    pallas_call x1, Pallas kernels, per_device(): pl.pallas_call(functools.partial(kernel, n, heads), out_shape=pltpu.VMEM(...  18.2 us
    unnamed x1, local copies, waits for them, and re-layouts  0.62 us

profile of v4, /device:TPU:0, one launch (start us, length us, event | category | flops | bytes accessed | tf_op | source)
XLA Modules:
  0.0 18.8 jit_solution(12148908984464435268)
XLA Ops:
  0.0 18.2 %shard_map.100 = bf16[32,4,128]{2,1,0:T(4,128)(2,1)S(1)} custom-call(bf16[4,128,128]{2,1,0:T(8,128)(2,1)} %mant_hbm.1, s32[4,1,128]{2,1,0:T(1,128)} %expo_hbm.1, s32[1,128]{1,0:T(1,128)} %bitcast.9, f32[1,128]{1,0:T(1,128)} %bitcast.10, f32[1,128]{1,0:T(1,128)} %bitcast.11, bf16[128,512]{1,0:T(8,128)(2,1)} %proj_hbm.1, bf16[4,128]{1,0:T(4,128)(2,1)} %bitcast.8, ...), custom_call_target="tpu_custom_call" | custom-call | tf_op jit(solution)/shard_map/pallas_call | solution.py:222
  18.2 0.6 %copy.12 = bf16[1,128,128]{2,1,0:T(8,128)(2,1)} copy(bf16[1,128,128]{2,1,0:T(8,128)(2,1)S(1)} %bitcast.7) | data formatting | bytes 65536
